TPU v7x, 512 devices: a whole 4x8x8 slice. The times are simulated.
512 devices in a mesh: recv: 32 (over x, z_lo, core), src: 16 (over y, z_hi).
Axes of the slice: x: 4, y: 8, z: 8 (z_hi: 2, z_lo: 4; z = z_hi * 4 + z_lo), core: 2. Of those that a mesh axis runs over, the one named last changes fastest.
Arguments:
- record: bfloat16 [512, 131072], P('recv', 'src'), may hold values from -41 to 41
- source_channel: int32 [32], replicated, may hold values from 0 to 511, as said below
- band_edges: int32 [32, 2], replicated, may hold values from 0 to 512, as said below
- offsets: int32 [16], replicated, may hold values from 0 to 5376, as said below
Outputs:
- virtual_gathers: float32 [32, 512, 256], P('src', 'recv')
Inputs may be any that keep to these rules, and one draw needn't show every extreme that they name: `source_channel`: the 32 channels are distinct. band_edges[s, 0] < band_edges[s, 1] for every source. `offsets`: window w lies inside time shard w.
All inputs are finite; a program needn't handle non-finite values.
Results may differ from a plain program's by a relative error of at most 0.0041.
Values may be sent and summed in bfloat16 or wider, within the bound.
No kernel may reach another device: no remote copies, remote signals or barrier semaphores. Data moves between devices by JAX's collectives and lax.ppermute only.
A program may use at most 64 MiB of HBM per device.

v0:
```python
import jax
import jax.numpy as jnp
from jax import lax
from jax.sharding import PartitionSpec as P

WL = 2560
L = 256
EPSILON = 1e-06


def whiten(segment):
    values = segment.astype(jnp.float32)
    spread = jnp.sqrt(jnp.mean(values * values, axis=-1, keepdims=True) + EPSILON)
    return (values / spread).astype(jnp.bfloat16)


def correlate_group(group_rows, recv_rows):
    seg_len = recv_rows.shape[1]
    row_count = group_rows.shape[0]
    source_part = group_rows[:, L // 2 : L // 2 + WL]
    zero_tail = jnp.zeros((row_count, seg_len + 1 - WL), jnp.bfloat16)
    padded = jnp.concatenate([source_part, zero_tail], axis=1)
    tiled = jnp.tile(padded, (1, L))[:, : L * seg_len].reshape(row_count, L, seg_len)
    return jnp.einsum("skt,rt->srk", tiled, recv_rows, preferred_element_type=jnp.float32)


def correlate(source_rows, recv_rows):
    row_count = source_rows.shape[0]
    group_size = 2
    grouped = source_rows.reshape(row_count // group_size, group_size, source_rows.shape[1])
    results = lax.map(lambda group_rows: correlate_group(group_rows, recv_rows), grouped)
    return results.reshape(row_count, recv_rows.shape[0], L)


def local(record, source_channel, band_edges, offsets):
    chan_dev = record.shape[0]
    seg_len = WL + L
    recv_index = lax.axis_index("recv")
    src_index = lax.axis_index("src")
    src_count = lax.axis_size("src")
    source_total = source_channel.shape[0]
    source_block = source_total // src_count
    window_start = lax.dynamic_index_in_dim(offsets, src_index, 0, keepdims=False)
    segment = lax.dynamic_slice(record, (jnp.int32(0), window_start), (chan_dev, seg_len))
    recv_rows = whiten(segment)
    channel_ids = recv_index * chan_dev + jnp.arange(chan_dev, dtype=jnp.int32)
    selector = (source_channel[:, None] == channel_ids[None, :]).astype(jnp.bfloat16)
    picked = jnp.dot(selector, segment, preferred_element_type=jnp.float32)
    source_raw = lax.psum(picked.astype(jnp.bfloat16), "recv")
    source_rows = whiten(source_raw)
    own_sources = lax.all_to_all(
        source_rows[:, None, :], "src", split_axis=0, concat_axis=1, tiled=True
    )
    initial = jnp.zeros((source_block, chan_dev, L), jnp.float32)
    shard_piece = lax.all_gather(recv_rows[None], "src", axis=0, tiled=True)

    def one_window(number, carried):
        recv_piece = lax.dynamic_index_in_dim(shard_piece, number, 0, keepdims=False)
        source_piece = lax.dynamic_index_in_dim(own_sources, number, 1, keepdims=False)
        return carried + correlate(source_piece, recv_piece)

    stacked = lax.fori_loop(0, shard_piece.shape[0], one_window, initial)
    factor = 1.0 / float(WL * src_count) ** 0.5
    own_channel = lax.dynamic_slice_in_dim(
        source_channel, src_index * source_block, source_block, 0
    )
    own_edges = lax.dynamic_slice_in_dim(band_edges, src_index * source_block, source_block, 0)
    in_band = (channel_ids[None, :] >= own_edges[:, 0:1]) & (
        channel_ids[None, :] < own_edges[:, 1:2]
    )
    in_band = in_band & (channel_ids[None, :] != own_channel[:, None])
    return jnp.where(in_band[:, :, None], stacked * factor, jnp.float32(0.0))


def solution(mesh):
    in_specs = (P("recv", "src"), P(), P(), P())
    out_specs = P("src", "recv", None)
    return jax.shard_map(local, mesh=mesh, in_specs=in_specs, out_specs=out_specs, check_vma=False)
```

profile of v0, /device:TPU:8, one launch (start us, length us, event | category | flops | bytes accessed | tf_op | source)
XLA Modules:
  0.0 639.9 jit_solution(3919369733604993040)
XLA Ops:
  16.1 281.3 %all-reduce.3.cloned.1.call-done = bf16[32,2816]{1,0:T(8,128)(2,1)} async-done(((bf16[32,2816]{1,0:T(8,128)(2,1)}), bf16[32,2816]{1,0:T(8,128)(2,1)}) %all-reduce.3.cloned.1.call-update) | async-done | bytes 180240 | tf_op jit(solution)/shard_map/psum | solution.py:49
  301.5 12.8 %all-to-all-start = ((bf16[16,2,2816]{2,1,0:T(2,128)(2,1)}), bf16[16,2,2816]{2,1,0:T(2,128)(2,1)S(1)}, u32[]{:S(2)}, u32[]{:S(2)}) async-start(bf16[16,2,2816]{2,1,0:T(2,128)(2,1)} %reshape.136), calls=%async_computation | async-start | bytes 360448 | tf_op jit(solution)/shard_map/all_to_all | solution.py:51
  314.4 12.5 %all-to-all-done = bf16[16,2,2816]{2,1,0:T(2,128)(2,1)S(1)} async-done(((bf16[16,2,2816]{2,1,0:T(2,128)(2,1)}), bf16[16,2,2816]{2,1,0:T(2,128)(2,1)S(1)}, u32[]{:S(2)}, u32[]{:S(2)}) %all-to-all-start) | async-done | bytes 180256 | tf_op jit(solution)/shard_map/all_to_all | solution.py:51
  328.2 303.5 %while.22 = (s32[]{:T(128)}, f32[2,16,256]{2,1,0:T(8,128)S(1)}, bf16[16,16,2816]{2,1,0:T(8,128)(2,1)}, bf16[2,16,2816]{2,0,1:T(2,128)(2,1)S(1)}, s32[]{:T(128)}, /*index=5*/bf16[]{:T(256)}, s32[]{:T(128)}) while((s32[]{:T(128)}, f32[2,16,256]{2,1,0:T(8,128)S(1)}, bf16[16,16,2816]{2,1,0:T(8,128)(2,1)}, ...), condition=%wide.region_4.5_spmd.clone, body=%wide.region_3.4_spmd.clone.sunk | while | flops 46153728 | bytes 23305828 | solution.py:62
  328.5 6.4 %reshape.139 = bf16[1442304]{0:T(1024)(128)(2,1)} reshape(bf16[2,256,2817]{2,1,0:T(8,128)(2,1)S(1)} %tile.30) | data formatting | bytes 5769216 | tf_op jit(solution)/shard_map/while
  334.9 5.8 tile.31
  347.5 6.4 %reshape.139 = bf16[1442304]{0:T(1024)(128)(2,1)} reshape(bf16[2,256,2817]{2,1,0:T(8,128)(2,1)S(1)} %tile.30) | data formatting | bytes 5769216 | tf_op jit(solution)/shard_map/while
  353.9 5.8 tile.31
  366.4 6.4 %reshape.139 = bf16[1442304]{0:T(1024)(128)(2,1)} reshape(bf16[2,256,2817]{2,1,0:T(8,128)(2,1)S(1)} %tile.30) | data formatting | bytes 5769216 | tf_op jit(solution)/shard_map/while
  372.9 5.8 tile.31
  385.4 6.4 %reshape.139 = bf16[1442304]{0:T(1024)(128)(2,1)} reshape(bf16[2,256,2817]{2,1,0:T(8,128)(2,1)S(1)} %tile.30) | data formatting | bytes 5769216 | tf_op jit(solution)/shard_map/while
  391.8 5.8 tile.31
  404.4 6.4 %reshape.139 = bf16[1442304]{0:T(1024)(128)(2,1)} reshape(bf16[2,256,2817]{2,1,0:T(8,128)(2,1)S(1)} %tile.30) | data formatting | bytes 5769216 | tf_op jit(solution)/shard_map/while
  410.8 5.8 tile.31
  423.4 6.4 %reshape.139 = bf16[1442304]{0:T(1024)(128)(2,1)} reshape(bf16[2,256,2817]{2,1,0:T(8,128)(2,1)S(1)} %tile.30) | data formatting | bytes 5769216 | tf_op jit(solution)/shard_map/while
  429.8 5.8 tile.31
  442.3 6.4 %reshape.139 = bf16[1442304]{0:T(1024)(128)(2,1)} reshape(bf16[2,256,2817]{2,1,0:T(8,128)(2,1)S(1)} %tile.30) | data formatting | bytes 5769216 | tf_op jit(solution)/shard_map/while
  448.7 5.8 tile.31
  461.3 6.4 %reshape.139 = bf16[1442304]{0:T(1024)(128)(2,1)} reshape(bf16[2,256,2817]{2,1,0:T(8,128)(2,1)S(1)} %tile.30) | data formatting | bytes 5769216 | tf_op jit(solution)/shard_map/while
  467.7 5.8 tile.31
  480.3 6.4 %reshape.139 = bf16[1442304]{0:T(1024)(128)(2,1)} reshape(bf16[2,256,2817]{2,1,0:T(8,128)(2,1)S(1)} %tile.30) | data formatting | bytes 5769216 | tf_op jit(solution)/shard_map/while
  486.7 5.8 tile.31
  499.2 6.4 %reshape.139 = bf16[1442304]{0:T(1024)(128)(2,1)} reshape(bf16[2,256,2817]{2,1,0:T(8,128)(2,1)S(1)} %tile.30) | data formatting | bytes 5769216 | tf_op jit(solution)/shard_map/while
  505.7 5.8 tile.31
  518.2 6.4 %reshape.139 = bf16[1442304]{0:T(1024)(128)(2,1)} reshape(bf16[2,256,2817]{2,1,0:T(8,128)(2,1)S(1)} %tile.30) | data formatting | bytes 5769216 | tf_op jit(solution)/shard_map/while
  524.6 5.8 tile.31
  537.2 6.4 %reshape.139 = bf16[1442304]{0:T(1024)(128)(2,1)} reshape(bf16[2,256,2817]{2,1,0:T(8,128)(2,1)S(1)} %tile.30) | data formatting | bytes 5769216 | tf_op jit(solution)/shard_map/while
  543.6 5.8 tile.31
  556.1 6.4 %reshape.139 = bf16[1442304]{0:T(1024)(128)(2,1)} reshape(bf16[2,256,2817]{2,1,0:T(8,128)(2,1)S(1)} %tile.30) | data formatting | bytes 5769216 | tf_op jit(solution)/shard_map/while
  575.1 6.4 %reshape.139 = bf16[1442304]{0:T(1024)(128)(2,1)} reshape(bf16[2,256,2817]{2,1,0:T(8,128)(2,1)S(1)} %tile.30) | data formatting | bytes 5769216 | tf_op jit(solution)/shard_map/while
  594.1 6.4 %reshape.139 = bf16[1442304]{0:T(1024)(128)(2,1)} reshape(bf16[2,256,2817]{2,1,0:T(8,128)(2,1)S(1)} %tile.30) | data formatting | bytes 5769216 | tf_op jit(solution)/shard_map/while
  613.1 6.4 %reshape.139 = bf16[1442304]{0:T(1024)(128)(2,1)} reshape(bf16[2,256,2817]{2,1,0:T(8,128)(2,1)S(1)} %tile.30) | data formatting | bytes 5769216 | tf_op jit(solution)/shard_map/while
  (128 shorter events, 143.3 us)
Async XLA Ops:
  7.4 8.7 %copy-start = (s32[32,2]{0,1:T(2,128)S(1)}, s32[32,2]{0,1:T(2,128)}, u32[]{:S(2)}) copy-start(s32[32,2]{0,1:T(2,128)} %param.8) | copy-start | bytes 772
  7.4 290.1 %all-reduce.3.cloned.1.call-start = ((), (), s32[]{:S(2)}) async-start(), calls=%async_computation.1 | async-start | bytes 360448 | tf_op jit(solution)/shard_map/psum | solution.py:49
  12.5 315.7 %all-gather.3.cloned.1.call-start = ((), (), s32[]{:S(2)}) async-start(), calls=%async_computation.2 | async-start | bytes 1531904 | tf_op jit(solution)/shard_map/all_gather | solution.py:55
  301.5 25.4 %all-to-all-start = ((bf16[16,2,2816]{2,1,0:T(2,128)(2,1)}), bf16[16,2,2816]{2,1,0:T(2,128)(2,1)S(1)}, u32[]{:S(2)}, u32[]{:S(2)}) async-start(bf16[16,2,2816]{2,1,0:T(2,128)(2,1)} %reshape.136), calls=%async_computation | async-start | bytes 360448 | tf_op jit(solution)/shard_map/all_to_all | solution.py:51
Sparse Core Ops, SparseCore 0:
  12.6 284.8 all-reduce.2
Sparse Core Ops, SparseCore 1:
  16.1 102.0 all-gather.2
where the time goes:
time: 641 us; the launch traced here: 640 us
  waiting for transfers between devices  294 us (46%)
  local copies, waits for them, and re-layouts  263 us (41%)
  matrix products  45.2 us (7%)
  between operations  16.8 us (3%)
  starting transfers between devices  12.9 us (2%)
  other arithmetic  7.37 us (1%)
    psum x1, waiting for transfers between devices, local(): source_raw = lax.psum(picked.astype(jnp.bfloat16), 'recv')  281 us
    while x16, local copies, waits for them, and re-layouts  103 us
    another operation x32, local copies, waits for them, and re-layouts, correlate_group(): jnp.tile(padded, (1, L))[:, :L * seg_len].reshape(row_count, L, seg_len)  96.1 us
    slice x16, local copies, waits for them, and re-layouts, correlate_group(): jnp.tile(padded, (1, L))[:, :L * seg_len].reshape(row_count, L, seg_len)  59.8 us
    dot_general x16, matrix products, correlate_group(): jnp.einsum('skt,rt->srk', tiled, recv_rows, preferred_element_type=jnp.fl...  43.4 us
    all_to_all x1, starting transfers between devices, local(): lax.all_to_all(source_rows[:, None, :], 'src', split_axis=0, concat_axis=...  12.8 us
  transfers between devices with their start and end apart: 3, of which 2 were waited for; matrix products, arithmetic and copies ran while one was open for 1% of the time, Pallas kernels for 0%

commit v1 on v0

--- a/solution.py
+++ b/solution.py
@@ -46,7 +46,7 @@
     channel_ids = recv_index * chan_dev + jnp.arange(chan_dev, dtype=jnp.int32)
     selector = (source_channel[:, None] == channel_ids[None, :]).astype(jnp.bfloat16)
     picked = jnp.dot(selector, segment, preferred_element_type=jnp.float32)
-    source_raw = lax.psum(picked.astype(jnp.bfloat16), "recv")
+    source_raw = jnp.sum(lax.all_gather(picked.astype(jnp.bfloat16), "recv"), axis=0)
     source_rows = whiten(source_raw)
     own_sources = lax.all_to_all(
         source_rows[:, None, :], "src", split_axis=0, concat_axis=1, tiled=True

time: 641 us -> 501 us (0.78)
  the two profiles are of different devices: /device:TPU:8 before, /device:TPU:2 now
where the time goes in v1:
time: 501 us; the launch traced here: 499 us
  local copies, waits for them, and re-layouts  263 us (52%)
  waiting for transfers between devices  154 us (31%)
  matrix products  45.2 us (9%)
  between operations  15.4 us (3%)
  other arithmetic  10.3 us (2%)
  starting transfers between devices  10.2 us (2%)
    while x16, local copies, waits for them, and re-layouts  103 us
    another operation x32, local copies, waits for them, and re-layouts, correlate_group(): jnp.tile(padded, (1, L))[:, :L * seg_len].reshape(row_count, L, seg_len)  96.1 us
    all_gather x1, waiting for transfers between devices, local(): lax.all_gather(picked.astype(jnp.bfloat16), 'recv')  69.7 us
    all_gather x1, waiting for transfers between devices, local(): shard_piece = lax.all_gather(recv_rows[None], 'src', axis=0, tiled=True)  69.2 us
    slice x16, local copies, waits for them, and re-layouts, correlate_group(): jnp.tile(padded, (1, L))[:, :L * seg_len].reshape(row_count, L, seg_len)  59.7 us
    dot_general x16, matrix products, correlate_group(): jnp.einsum('skt,rt->srk', tiled, recv_rows, preferred_element_type=jnp.fl...  43.4 us
    all_to_all x1, waiting for transfers between devices, local(): lax.all_to_all(source_rows[:, None, :], 'src', split_axis=0, concat_axis=...  15.4 us
    all_to_all x1, starting transfers between devices, local(): lax.all_to_all(source_rows[:, None, :], 'src', split_axis=0, concat_axis=...  10.2 us
  transfers between devices with their start and end apart: 3, of which 3 were waited for; matrix products, arithmetic and copies ran while one was open for 2% of the time, Pallas kernels for 0%

profile of v1, /device:TPU:2, one launch (start us, length us, event | category | flops | bytes accessed | tf_op | source)
XLA Modules:
  0.0 499.4 jit_solution(7160993454290861838)
XLA Ops:
  15.3 69.7 %all-gather.7.cloned.1.call-done = bf16[1024,2816]{1,0:T(8,128)(2,1)} async-done(((bf16[32,2816]{1,0:T(8,128)(2,1)}), bf16[1024,2816]{1,0:T(8,128)(2,1)}) %all-gather.7.cloned.1.call-update) | async-done | bytes 5767184 | tf_op jit(solution)/shard_map/all_gather | solution.py:49
  91.9 10.2 %all-to-all-start = ((bf16[16,2,2816]{2,1,0:T(2,128)(2,1)}), bf16[16,2,2816]{2,1,0:T(2,128)(2,1)S(1)}, u32[]{:S(2)}, u32[]{:S(2)}) async-start(bf16[16,2,2816]{2,1,0:T(2,128)(2,1)} %reshape.174), calls=%async_computation | async-start | bytes 360448 | tf_op jit(solution)/shard_map/all_to_all | solution.py:51
  102.2 15.4 %all-to-all-done = bf16[16,2,2816]{2,1,0:T(2,128)(2,1)S(1)} async-done(((bf16[16,2,2816]{2,1,0:T(2,128)(2,1)}), bf16[16,2,2816]{2,1,0:T(2,128)(2,1)S(1)}, u32[]{:S(2)}, u32[]{:S(2)}) %all-to-all-start) | async-done | bytes 180256 | tf_op jit(solution)/shard_map/all_to_all | solution.py:51
  118.9 69.2 %all-gather.5.cloned.1.call-done = bf16[256,2816]{1,0:T(8,128)(2,1)} async-done(((bf16[16,2816]{1,0:T(8,128)(2,1)}), bf16[256,2816]{1,0:T(8,128)(2,1)}) %all-gather.5.cloned.1.call-update) | async-done | bytes 1441808 | tf_op jit(solution)/shard_map/all_gather | solution.py:55
  188.1 303.8 %while.22 = (s32[]{:T(128)}, f32[2,16,256]{2,1,0:T(8,128)S(1)}, bf16[16,16,2816]{2,1,0:T(8,128)(2,1)}, bf16[2,16,2816]{2,0,1:T(2,128)(2,1)S(1)}, s32[]{:T(128)}, /*index=5*/bf16[]{:T(256)}, s32[]{:T(128)}) while((s32[]{:T(128)}, f32[2,16,256]{2,1,0:T(8,128)S(1)}, bf16[16,16,2816]{2,1,0:T(8,128)(2,1)}, ...), condition=%wide.region_4.5_spmd.clone, body=%wide.region_3.4_spmd.clone.sunk | while | flops 46153728 | bytes 23305828 | solution.py:62
  188.4 6.5 %reshape.177 = bf16[1442304]{0:T(1024)(128)(2,1)} reshape(bf16[2,256,2817]{2,1,0:T(8,128)(2,1)S(1)} %tile.30) | data formatting | bytes 5769216 | tf_op jit(solution)/shard_map/while
  194.8 5.8 %tile.31 = bf16[2,721152]{1,0:T(2,128)(2,1)S(1)} reshape(bf16[1442304]{0:T(1024)(128)(2,1)} %reshape.177) | data formatting | bytes 5769216 | tf_op jit(solution)/shard_map/while/body/eval_jaxpr/while/body/eval_jaxpr/tile | solution.py:23
  207.3 6.5 %reshape.177 = bf16[1442304]{0:T(1024)(128)(2,1)} reshape(bf16[2,256,2817]{2,1,0:T(8,128)(2,1)S(1)} %tile.30) | data formatting | bytes 5769216 | tf_op jit(solution)/shard_map/while
  213.8 5.8 %tile.31 = bf16[2,721152]{1,0:T(2,128)(2,1)S(1)} reshape(bf16[1442304]{0:T(1024)(128)(2,1)} %reshape.177) | data formatting | bytes 5769216 | tf_op jit(solution)/shard_map/while/body/eval_jaxpr/while/body/eval_jaxpr/tile | solution.py:23
  226.3 6.5 %reshape.177 = bf16[1442304]{0:T(1024)(128)(2,1)} reshape(bf16[2,256,2817]{2,1,0:T(8,128)(2,1)S(1)} %tile.30) | data formatting | bytes 5769216 | tf_op jit(solution)/shard_map/while
  232.8 5.8 %tile.31 = bf16[2,721152]{1,0:T(2,128)(2,1)S(1)} reshape(bf16[1442304]{0:T(1024)(128)(2,1)} %reshape.177) | data formatting | bytes 5769216 | tf_op jit(solution)/shard_map/while/body/eval_jaxpr/while/body/eval_jaxpr/tile | solution.py:23
  245.3 6.5 %reshape.177 = bf16[1442304]{0:T(1024)(128)(2,1)} reshape(bf16[2,256,2817]{2,1,0:T(8,128)(2,1)S(1)} %tile.30) | data formatting | bytes 5769216 | tf_op jit(solution)/shard_map/while
  251.8 5.8 %tile.31 = bf16[2,721152]{1,0:T(2,128)(2,1)S(1)} reshape(bf16[1442304]{0:T(1024)(128)(2,1)} %reshape.177) | data formatting | bytes 5769216 | tf_op jit(solution)/shard_map/while/body/eval_jaxpr/while/body/eval_jaxpr/tile | solution.py:23
  264.3 6.5 %reshape.177 = bf16[1442304]{0:T(1024)(128)(2,1)} reshape(bf16[2,256,2817]{2,1,0:T(8,128)(2,1)S(1)} %tile.30) | data formatting | bytes 5769216 | tf_op jit(solution)/shard_map/while
  270.8 5.8 %tile.31 = bf16[2,721152]{1,0:T(2,128)(2,1)S(1)} reshape(bf16[1442304]{0:T(1024)(128)(2,1)} %reshape.177) | data formatting | bytes 5769216 | tf_op jit(solution)/shard_map/while/body/eval_jaxpr/while/body/eval_jaxpr/tile | solution.py:23
  283.3 6.5 %reshape.177 = bf16[1442304]{0:T(1024)(128)(2,1)} reshape(bf16[2,256,2817]{2,1,0:T(8,128)(2,1)S(1)} %tile.30) | data formatting | bytes 5769216 | tf_op jit(solution)/shard_map/while
  302.3 6.5 %reshape.177 = bf16[1442304]{0:T(1024)(128)(2,1)} reshape(bf16[2,256,2817]{2,1,0:T(8,128)(2,1)S(1)} %tile.30) | data formatting | bytes 5769216 | tf_op jit(solution)/shard_map/while
  321.3 6.5 %reshape.177 = bf16[1442304]{0:T(1024)(128)(2,1)} reshape(bf16[2,256,2817]{2,1,0:T(8,128)(2,1)S(1)} %tile.30) | data formatting | bytes 5769216 | tf_op jit(solution)/shard_map/while
  327.7 5.8 %tile.31 = bf16[2,721152]{1,0:T(2,128)(2,1)S(1)} reshape(bf16[1442304]{0:T(1024)(128)(2,1)} %reshape.177) | data formatting | bytes 5769216 | tf_op jit(solution)/shard_map/while/body/eval_jaxpr/while/body/eval_jaxpr/tile | solution.py:23
  340.3 6.5 %reshape.177 = bf16[1442304]{0:T(1024)(128)(2,1)} reshape(bf16[2,256,2817]{2,1,0:T(8,128)(2,1)S(1)} %tile.30) | data formatting | bytes 5769216 | tf_op jit(solution)/shard_map/while
  346.7 5.8 %tile.31 = bf16[2,721152]{1,0:T(2,128)(2,1)S(1)} reshape(bf16[1442304]{0:T(1024)(128)(2,1)} %reshape.177) | data formatting | bytes 5769216 | tf_op jit(solution)/shard_map/while/body/eval_jaxpr/while/body/eval_jaxpr/tile | solution.py:23
  359.3 6.5 %reshape.177 = bf16[1442304]{0:T(1024)(128)(2,1)} reshape(bf16[2,256,2817]{2,1,0:T(8,128)(2,1)S(1)} %tile.30) | data formatting | bytes 5769216 | tf_op jit(solution)/shard_map/while
  378.3 6.5 %reshape.177 = bf16[1442304]{0:T(1024)(128)(2,1)} reshape(bf16[2,256,2817]{2,1,0:T(8,128)(2,1)S(1)} %tile.30) | data formatting | bytes 5769216 | tf_op jit(solution)/shard_map/while
  384.7 5.8 %tile.31 = bf16[2,721152]{1,0:T(2,128)(2,1)S(1)} reshape(bf16[1442304]{0:T(1024)(128)(2,1)} %reshape.177) | data formatting | bytes 5769216 | tf_op jit(solution)/shard_map/while/body/eval_jaxpr/while/body/eval_jaxpr/tile | solution.py:23
  397.2 6.5 %reshape.177 = bf16[1442304]{0:T(1024)(128)(2,1)} reshape(bf16[2,256,2817]{2,1,0:T(8,128)(2,1)S(1)} %tile.30) | data formatting | bytes 5769216 | tf_op jit(solution)/shard_map/while
  403.7 5.8 %tile.31 = bf16[2,721152]{1,0:T(2,128)(2,1)S(1)} reshape(bf16[1442304]{0:T(1024)(128)(2,1)} %reshape.177) | data formatting | bytes 5769216 | tf_op jit(solution)/shard_map/while/body/eval_jaxpr/while/body/eval_jaxpr/tile | solution.py:23
  416.2 6.5 %reshape.177 = bf16[1442304]{0:T(1024)(128)(2,1)} reshape(bf16[2,256,2817]{2,1,0:T(8,128)(2,1)S(1)} %tile.30) | data formatting | bytes 5769216 | tf_op jit(solution)/shard_map/while
  435.2 6.5 %reshape.177 = bf16[1442304]{0:T(1024)(128)(2,1)} reshape(bf16[2,256,2817]{2,1,0:T(8,128)(2,1)S(1)} %tile.30) | data formatting | bytes 5769216 | tf_op jit(solution)/shard_map/while
  441.7 5.8 %tile.31 = bf16[2,721152]{1,0:T(2,128)(2,1)S(1)} reshape(bf16[1442304]{0:T(1024)(128)(2,1)} %reshape.177) | data formatting | bytes 5769216 | tf_op jit(solution)/shard_map/while/body/eval_jaxpr/while/body/eval_jaxpr/tile | solution.py:23
  454.2 6.5 %reshape.177 = bf16[1442304]{0:T(1024)(128)(2,1)} reshape(bf16[2,256,2817]{2,1,0:T(8,128)(2,1)S(1)} %tile.30) | data formatting | bytes 5769216 | tf_op jit(solution)/shard_map/while
  460.7 5.8 %tile.31 = bf16[2,721152]{1,0:T(2,128)(2,1)S(1)} reshape(bf16[1442304]{0:T(1024)(128)(2,1)} %reshape.177) | data formatting | bytes 5769216 | tf_op jit(solution)/shard_map/while/body/eval_jaxpr/while/body/eval_jaxpr/tile | solution.py:23
  473.2 6.5 %reshape.177 = bf16[1442304]{0:T(1024)(128)(2,1)} reshape(bf16[2,256,2817]{2,1,0:T(8,128)(2,1)S(1)} %tile.30) | data formatting | bytes 5769216 | tf_op jit(solution)/shard_map/while
  (130 shorter events, 151.8 us)
Async XLA Ops:
  6.5 8.7 %copy-start = (s32[32,2]{0,1:T(2,128)S(1)}, s32[32,2]{0,1:T(2,128)}, u32[]{:S(2)}) copy-start(s32[32,2]{0,1:T(2,128)} %param.8) | copy-start | bytes 772
  6.5 78.5 %all-gather.7.cloned.1.call-start = ((), (), s32[]{:S(2)}) async-start(), calls=%async_computation.2 | async-start | bytes 5947392 | tf_op jit(solution)/shard_map/all_gather | solution.py:49
  11.6 176.5 %all-gather.5.cloned.1.call-start = ((), (), s32[]{:S(2)}) async-start(), calls=%async_computation.1 | async-start | bytes 1531904 | tf_op jit(solution)/shard_map/all_gather | solution.py:55
  91.9 25.6 %all-to-all-start = ((bf16[16,2,2816]{2,1,0:T(2,128)(2,1)}), bf16[16,2,2816]{2,1,0:T(2,128)(2,1)S(1)}, u32[]{:S(2)}, u32[]{:S(2)}) async-start(bf16[16,2,2816]{2,1,0:T(2,128)(2,1)} %reshape.174), calls=%async_computation | async-start | bytes 360448 | tf_op jit(solution)/shard_map/all_to_all | solution.py:51
Sparse Core Ops, SparseCore 0:
  11.7 73.2 all-gather.6
  88.2 99.8 all-gather.4
